TPU v7x, 128 devices: a whole 4x4x4 slice. The times are simulated.
128 devices in a mesh: gx: 8 (over y, x_hi), gy: 16 (over x_lo, z, core).
Axes of the slice: x: 4 (x_hi: 2, x_lo: 2; x = x_hi * 2 + x_lo), y: 4, z: 4, core: 2. Of those that a mesh axis runs over, the one named last changes fastest.
Arguments:
- charges: float32 [512, 256, 128], P('gx', 'gy'), may hold values from -6 to 6
- kernel_fine: bfloat16 [9, 9, 9], replicated, may hold values from -0.21875 to 0.21875
- kernel_mid: bfloat16 [9, 9, 9], replicated, may hold values from -0.109375 to 0.109375
- kernel_coarse: bfloat16 [9, 9, 9], replicated, may hold values from -0.0546875 to 0.0546875
Outputs:
- potential: float32 [512, 256, 128], P('gx', 'gy')
All inputs are finite; a program needn't handle non-finite values.
Results may differ from a plain program's by a relative error of at most 0.0028.
Values may be sent and summed in bfloat16 or wider, within the bound.
A program may use at most 128 MiB of HBM per device.

v0:
```python
import functools

import jax
import jax.numpy as jnp
import numpy as np
from jax import lax
from jax.experimental import pallas as pl
from jax.experimental.pallas import tpu as pltpu
from jax.sharding import PartitionSpec as P

bf16, f32 = jnp.bfloat16, jnp.float32
MESH = pl.DeviceIdType.MESH
TAPS = {-3: -0.0625, -1: 0.5625, 0: 1.0, 1: 0.5625, 3: -0.0625}
LEVELS = ((128, 1, 9), (64, 2, 10), (32, 4, 12))
NEAR = ((0, -1), (0, 1), (-1, 0), (1, 0), (-1, -1), (-1, 1), (1, -1), (1, 1))
FAR = tuple((i, j) for i in (-1, 0, 1) for j in (-2, -1, 0, 1, 2) if (i, j) != (0, 0))


def taps_matrix(fine, coarse):
    spacing = np.asarray(fine)[:, None] - 2 * np.asarray(coarse)[None, :]
    matrix = np.zeros(spacing.shape, np.float32)
    for offset, factor in TAPS.items():
        matrix[spacing == offset] = factor
    return matrix


def constants():
    rz = taps_matrix(range(128), range(64))
    block_z = np.kron(np.eye(2, dtype=np.float32), rz)
    rz_mid = taps_matrix(range(64), range(32))
    to_coarse = np.kron(taps_matrix(range(-4, 10), range(4)), rz_mid)
    to_mid = np.concatenate([to_coarse[128 * m:128 * m + 128].T for m in range(7)])
    pieces = {}

    def wide(matrix):
        return np.pad(matrix, ((0, 0), (0, 128 - matrix.shape[1])))

    mid_rows = [r - 8 for r in range(48)]
    pieces["block_z"] = block_z
    pieces["spread_z"] = np.concatenate([block_z.T[:, :128], block_z.T[:, 128:]])
    pieces["to_coarse"] = to_coarse
    pieces["to_mid"] = to_mid
    rx = taps_matrix(range(64), mid_rows).T
    pieces["rx"] = np.concatenate([rx, rx], axis=1)
    rc = taps_matrix(mid_rows, range(16)).T
    pieces["rc"] = wide(np.concatenate([rc, rc], axis=1))
    pc = taps_matrix([o - 1 for o in range(48)], [i - 2 for i in range(32)])
    pc[35:] = 0.0
    pieces["pc"] = wide(np.concatenate([pc, pc], axis=1))
    px = taps_matrix(range(64), [o - 1 for o in range(48)])
    px[:, 35:] = 0.0
    pieces["px"] = wide(np.concatenate([px, px], axis=1))
    at, rows = {}, 0
    for name, piece in pieces.items():
        at[name] = (rows, piece.shape[0])
        rows += piece.shape[0]
    return np.concatenate(list(pieces.values())), at


TABLE, AT = constants()


def high_low(value):
    high = value.astype(bf16)
    return high, (value - high.astype(f32)).astype(bf16)


def dot(a, b):
    return jnp.dot(a, b, preferred_element_type=f32)


def toeplitz(kernel, base, table, level, first):
    cells, blocks, rows = LEVELS[level]
    width = 128 * blocks
    tap = lax.broadcasted_iota(jnp.int32, (9, width), 0)
    lane = lax.broadcasted_iota(jnp.int32, (9, width), 1)
    target = cells * (lane // 128) + 4 - tap
    place = jnp.where((lane - target) % 128 == 0, 1.0, 0.0).astype(bf16)
    base[...] = jnp.zeros_like(base)
    for dx in range(9):
        placed = dot(kernel[dx], place)
        for b in range(blocks):
            base[dx, b:b + 9, :] += placed[:, 128 * b:128 * b + 128]
    row = lax.broadcasted_iota(jnp.int32, (8, 128), 0)
    column = lax.broadcasted_iota(jnp.int32, (8, 128), 1) % cells
    top = jnp.abs(row - column) <= 4
    bottom = jnp.abs(row + cells - 8 - column) <= 4
    for dx in range(9):
        for e in range(rows):
            line = jnp.broadcast_to(base[dx, e:e + 1, :], (cells, 128))
            rolled = pltpu.roll(line, 0, 1, stride=1, stride_axis=0)
            band = jnp.concatenate(
                [jnp.where(top, rolled[:8], 0.0), rolled[8:cells - 8], jnp.where(bottom, rolled[cells - 8:], 0.0)], axis=0)
            table[dx, first + e * cells:first + (e + 1) * cells, :] = band.astype(bf16)
    if first:
        end = first + rows * cells
        for dx in range(9):
            table[dx, 0:first, :] = jnp.zeros((first, 128), bf16)
            table[dx, end:end + first, :] = jnp.zeros((first, 128), bf16)


def wide_table(table, dx, depth):
    return jnp.concatenate([table[dx, 128:128 + depth, :], table[dx, 0:depth, :]], axis=1)


def body(sizes, c_hbm, kf, km, kc, const_hbm, out,
         c, const, field, base_f, base_m, base_c, tab_f, tab_m, tab_c,
         v_in, v_ed, fine, y_s, y_r, x_s, x_r, k_s, k_r, m_s, my_r, mx_r, mk_r,
         mid, coarse_s, coarse_r, coarse, u_ref,
         load_sem, fs_sem, fr_sem, ms_sem, mr_sem, cs_sem, cr_sem):
    gx, gy = lax.axis_index("gx"), lax.axis_index("gy")
    nx, ny = sizes

    def device(i, j):
        return (lax.rem(gx + i + nx, nx), lax.rem(gy + j + ny, ny))

    def from_inside(i, j):
        x, y = gx - i, gy - j
        return (x >= 0) & (x < nx) & (y >= 0) & (y < ny)

    def inside_columns(matrix, period, first, end):
        place = lax.broadcasted_iota(jnp.int32, matrix.shape, 1) % period
        keep = ((place >= first) | (gx > 0)) & ((place < end) | (gx < nx - 1))
        return jnp.where(keep, matrix.astype(f32), 0.0).astype(bf16)

    def inside_y(value, place):
        if place == 0:
            return value
        return jnp.where(gy > 0 if place < 0 else gy < ny - 1, value, 0.0)

    load_c = pltpu.make_async_copy(c_hbm, c, load_sem.at[0])
    load_k = pltpu.make_async_copy(const_hbm, const, load_sem.at[1])
    load_c.start()
    load_k.start()
    barrier = pltpu.get_barrier_semaphore()
    for i, j in FAR:
        pl.semaphore_signal(barrier, inc=1, device_id=device(i, j), device_id_type=MESH)

    def table(name, width=128):
        start, rows = AT[name]
        return const[start:start + rows, 0:width]

    toeplitz(kf, base_f, tab_f, 0, 128)
    load_c.wait()
    for y in range(16):
        for b in range(8):
            field[4 + y, 8 + 8 * b:16 + 8 * b, :] = c[pl.ds(128 * b + y, 8, stride=16), :]
    for d, y0 in ((0, 0), (1, 12)):
        for y in range(4):
            y_s[d, y] = field[4 + y0 + y, 8:72, :].astype(bf16)
    for d, x0 in ((0, 0), (1, 60)):
        for x in range(4):
            x_s[d, x] = c[16 * (x0 + x):16 * (x0 + x) + 16, :].astype(bf16)
    for n, (i, j) in enumerate(NEAR[4:]):
        r0, y0 = (8 if i < 0 else 64), (4 if j < 0 else 16)
        for h in range(2):
            k_s[n, 16 * h:16 * h + 16, :] = jnp.concatenate(
                [field[y0 + 2 * h, r0:r0 + 8, :], field[y0 + 2 * h + 1, r0:r0 + 8, :]], axis=0).astype(bf16)

    load_k.wait()

    def along_y(row):
        total = None
        for offset, factor in TAPS.items():
            y = 2 * row + offset
            if 0 <= y < 16:
                term = factor * field[4 + y, 8:72, :]
                total = term if total is None else total + term
        return jnp.zeros((64, 128), f32) if total is None else total

    highs, lows = [], []
    for p in range(-1, 5):
        he, le = high_low(along_y(2 * p))
        ho, lo = high_low(along_y(2 * p + 1))
        highs.append(jnp.concatenate([he, ho], axis=1))
        lows.append(jnp.concatenate([le, lo], axis=1))
    shares = dot(jnp.concatenate(highs, axis=0), table("block_z")) + dot(jnp.concatenate(lows, axis=0), table("block_z"))
    split = []
    for p in range(6):
        high, low = high_low(shares[64 * p:64 * p + 64])
        split.append(jnp.concatenate([high, low], axis=0))
    share = dot(table("rx"), jnp.concatenate(split, axis=1))
    mid[...] = jnp.zeros_like(mid)
    mid[0:48, 256:1024] = share
    m_s[...] = share.astype(bf16)

    pl.semaphore_wait(barrier, len(FAR))
    sends = []

    def send(source, target, send_sem, recv_sem, i, j):
        copy = pltpu.make_async_remote_copy(
            src_ref=source, dst_ref=target, send_sem=send_sem, recv_sem=recv_sem,
            device_id=device(i, j), device_id_type=MESH)
        copy.start()
        return copy

    fine_copies, mid_copies = [], []
    for n, (i, j) in enumerate(NEAR):
        if i == 0:
            pair = (m_s.at[:, 0:512] if j < 0 else m_s.at[:, 256:768], my_r.at[n])
        elif j == 0:
            pair = (m_s.at[0:16, :] if i < 0 else m_s.at[32:48, :], mx_r.at[n - 2])
        else:
            rows = pl.ds(0, 16) if i < 0 else pl.ds(32, 16)
            columns = pl.ds(0, 512) if j < 0 else pl.ds(256, 512)
            pair = (m_s.at[rows, columns], mk_r.at[n - 4])
        mid_copies.append(send(*pair, ms_sem.at[n], mr_sem.at[n], i, j))
        if i == 0:
            pair = (y_s.at[n], y_r.at[n])
        elif j == 0:
            pair = (x_s.at[n - 2], x_r.at[n - 2])
        else:
            pair = (k_s.at[n - 4], k_r.at[n - 4])
        fine_copies.append(send(*pair, fs_sem.at[n], fr_sem.at[n], i, j))

    toeplitz(km, base_m, tab_m, 1, 128)
    toeplitz(kc, base_c, tab_c, 2, 0)

    def fill_inside(rows):
        for dx in range(9):
            for y in rows:
                v_in[dx, y] = field[y, 12 + dx:60 + dx, :].astype(bf16)

    def fine_inside(pairs):
        weights = jnp.concatenate([wide_table(tab_f, dx, 1280) for dx in range(9)], axis=0)
        left = jnp.concatenate(
            [jnp.concatenate([v_in[dx, 2 * q + k] for dx in range(9) for k in range(10)], axis=1) for q in pairs], axis=0)
        result = dot(left, weights)
        for n, q in enumerate(pairs):
            for k in range(2):
                fine[2 * q + k, 8:56, :] = result[48 * n:48 * n + 48, 128 * k:128 * k + 128]

    fill_inside(range(4, 20))
    fine_inside((2, 3, 4, 5))

    for n, (i, j) in enumerate(NEAR):
        mid_copies[n].wait_recv()
    for n, (i, j) in enumerate(NEAR):
        inside = from_inside(i, j)
        got = my_r[n] if i == 0 else mx_r[n - 2] if j == 0 else mk_r[n - 4]
        got = jnp.where(inside, got.astype(f32), 0.0)
        r0, rows = (0, 48) if i == 0 else (32, 16) if i < 0 else (0, 16)
        l0, lanes = (256, 768) if j == 0 else (768, 512) if j < 0 else (0, 512)
        mid[r0:r0 + rows, l0:l0 + lanes] += got
    @pl.when(gx == 0)
    def _():
        mid[0:8, :] = jnp.zeros((8, 1280), f32)

    @pl.when(gx == nx - 1)
    def _():
        mid[40:48, :] = jnp.zeros((8, 1280), f32)

    @pl.when(gy == 0)
    def _():
        mid[0:48, 0:384] = jnp.zeros((48, 384), f32)

    @pl.when(gy == ny - 1)
    def _():
        mid[0:48, 896:1280] = jnp.zeros((48, 384), f32)

    high, low = high_low(mid[0:48, 128:1024])
    shrunk = dot(table("rc", 96), jnp.concatenate([high, low], axis=0))
    high, low = high_low(shrunk)
    own = dot(jnp.concatenate([high, low], axis=0), table("to_coarse"))
    own = (own[0:16] + own[16:32]).astype(bf16)
    coarse_s[...] = own
    coarse_copies = [send(coarse_s, coarse_r.at[n], cs_sem.at[n], cr_sem.at[n], i, j) for n, (i, j) in enumerate(FAR)]

    for n in range(2):
        fine_copies[n].wait_recv()
        inside = from_inside(*NEAR[n])
        for y in range(4):
            field[(20 if n == 0 else 0) + y, 8:72, :] = jnp.where(inside, y_r[n, y].astype(f32), 0.0)
    fill_inside((0, 1, 2, 3, 20, 21, 22, 23))
    fine_inside((0, 1, 6, 7))
    for n in range(2, 4):
        fine_copies[n].wait_recv()
        inside = from_inside(*NEAR[n])
        for x in range(4):
            got = jnp.where(inside, x_r[n - 2, x].astype(f32), 0.0)
            for y in range(2):
                for k in range(8):
                    row = (72 if n == 2 else 4) + x
                    field[4 + 8 * y + k, row:row + 1, :] = got[8 * y + k:8 * y + k + 1, :]
    for n in range(4, 8):
        fine_copies[n].wait_recv()
        i, j = NEAR[n]
        inside = from_inside(i, j)
        r0, y0 = (72 if i < 0 else 0), (20 if j < 0 else 0)
        for h in range(2):
            got = jnp.where(inside, k_r[n - 4, 16 * h:16 * h + 16, :].astype(f32), 0.0)
            field[y0 + 2 * h, r0:r0 + 8, :] = got[0:8]
            field[y0 + 2 * h + 1, r0:r0 + 8, :] = got[8:16]
    for dx in range(9):
        for y in range(24):
            v_ed[dx, y] = jnp.concatenate(
                [field[y, 4 + dx:12 + dx, :], field[y, 60 + dx:68 + dx, :]], axis=0).astype(bf16)
    weights = jnp.concatenate([wide_table(tab_f, dx, 1280) for dx in range(9)], axis=0)
    left = jnp.concatenate(
        [jnp.concatenate([v_ed[dx, 2 * q + k] for dx in range(9) for k in range(10)], axis=1) for q in range(8)], axis=0)
    result = dot(left, weights)
    for q in range(8):
        for k in range(2):
            piece = result[16 * q:16 * q + 16, 128 * k:128 * k + 128]
            fine[2 * q + k, 0:8, :] = piece[0:8]
            fine[2 * q + k, 56:64, :] = piece[8:16]

    weights = jnp.concatenate([wide_table(tab_m, dx, 768) for dx in range(9)], axis=0)
    shifted = [mid[3 + dx:51 + dx, :].astype(bf16) for dx in range(9)]
    left = jnp.concatenate(
        [jnp.concatenate([shifted[dx][:, 256 * g:256 * g + 768] for dx in range(9)], axis=1) for g in range(3)], axis=0)
    mid_potential = dot(left, weights)

    coarse[48:56, :] = jnp.zeros((8, 640), f32)
    coarse[16:32, 256:384] = own.astype(f32)
    for n, (i, j) in enumerate(FAR):
        coarse_copies[n].wait_recv()
        coarse[16 - 16 * i:32 - 16 * i, 256 - 128 * j:384 - 128 * j] = jnp.where(
            from_inside(i, j), coarse_r[n].astype(f32), 0.0)
    weights = jnp.concatenate([tab_c[dx] for dx in range(9)], axis=0)
    shifted = [coarse[10 + dx:42 + dx, :].astype(bf16) for dx in range(9)]
    left = jnp.concatenate(
        [jnp.concatenate([shifted[dx][:, 128 * q:128 * q + 384] for dx in range(9)], axis=1) for q in range(3)], axis=0)
    coarse_potential = dot(left, weights)
    split = []
    for q in range(3):
        high, low = high_low(inside_y(coarse_potential[32 * q:32 * q + 32], q - 1))
        split.append(jnp.concatenate([high, low], axis=0))
    spread = dot(inside_columns(table("pc", 64), 32, 2, 18), jnp.concatenate(split, axis=1))
    high, low = high_low(spread)
    spread = jnp.concatenate([high, low], axis=0)
    to_mid = AT["to_mid"][0]
    split = []
    for p in range(-1, 5):
        g, h = (p + 1) // 2, (p + 1) % 2
        total = mid_potential[48 * g:48 * g + 48, 128 * h:128 * h + 128]
        for q in (-1, 0, 1):
            m = p - 4 * q + 2
            if 0 <= m < 7:
                part = dot(spread[:, 128 * (q + 1):128 * (q + 1) + 128], const[to_mid + 128 * m:to_mid + 128 * m + 128, :])
                total = total + (part[0:48] + part[48:96])
        high, low = high_low(inside_y(total, -1 if p < 0 else 1 if p > 3 else 0))
        split.append(jnp.concatenate([high, low], axis=0))
    along_x = dot(inside_columns(table("px", 96), 48, 1, 33), jnp.concatenate(split, axis=1))
    highs, lows = [], []
    for p in range(6):
        high, low = high_low(along_x[:, 128 * p:128 * p + 128])
        highs.append(high)
        lows.append(low)
    spread_z = AT["spread_z"][0]
    weights = jnp.concatenate([const[spread_z:spread_z + 128, :], const[spread_z + 128:spread_z + 256, :]], axis=1)
    along_z = dot(jnp.concatenate(highs, axis=0), weights) + dot(jnp.concatenate(lows, axis=0), weights)
    for p in range(6):
        for k in range(2):
            u_ref[2 * p + k] = along_z[64 * p:64 * p + 64, 128 * k:128 * k + 128]
    for b in range(8):
        even = fine[2 * b] + u_ref[b + 2]
        odd = fine[2 * b + 1] + (0.5625 * (u_ref[b + 2] + u_ref[b + 3]) - 0.0625 * (u_ref[b + 1] + u_ref[b + 4]))
        for x in range(8):
            out[pl.ds(128 * x + 2 * b, 8, stride=16), :] = even[8 * x:8 * x + 8]
            out[pl.ds(128 * x + 2 * b + 1, 8, stride=16), :] = odd[8 * x:8 * x + 8]
    for copy in fine_copies + mid_copies + coarse_copies:
        copy.wait_send()


def solution(mesh):
    sizes = (mesh.shape["gx"], mesh.shape["gy"])
    vmem, dma = pltpu.VMEM, pltpu.SemaphoreType.DMA
    in_vmem, anywhere = pl.BlockSpec(memory_space=pltpu.VMEM), pl.BlockSpec(memory_space=pl.ANY)

    def local(charges, kernel_fine, kernel_mid, kernel_coarse):
        call = pl.pallas_call(
            functools.partial(body, sizes),
            out_shape=jax.ShapeDtypeStruct((1024, 128), f32),
            in_specs=[anywhere, in_vmem, in_vmem, in_vmem, anywhere],
            out_specs=in_vmem,
            scratch_shapes=[
                vmem((1024, 128), f32), vmem(TABLE.shape, bf16), vmem((24, 80, 128), f32),
                vmem((9, 16, 128), f32), vmem((9, 16, 128), f32), vmem((9, 16, 128), f32),
                vmem((9, 1408, 128), bf16), vmem((9, 896, 128), bf16), vmem((9, 384, 128), bf16),
                vmem((9, 24, 48, 128), bf16), vmem((9, 24, 16, 128), bf16), vmem((16, 64, 128), f32),
                vmem((2, 4, 64, 128), bf16), vmem((2, 4, 64, 128), bf16),
                vmem((2, 4, 16, 128), bf16), vmem((2, 4, 16, 128), bf16),
                vmem((4, 32, 128), bf16), vmem((4, 32, 128), bf16),
                vmem((48, 768), bf16), vmem((2, 48, 512), bf16), vmem((2, 16, 768), bf16), vmem((4, 16, 512), bf16),
                vmem((64, 1280), f32), vmem((16, 128), bf16), vmem((14, 16, 128), bf16), vmem((56, 640), f32),
                vmem((12, 64, 128), f32),
                dma((2,)), dma((8,)), dma((8,)), dma((8,)), dma((8,)), dma((14,)), dma((14,)),
            ],
            compiler_params=pltpu.CompilerParams(
                collective_id=0, has_side_effects=True, vmem_limit_bytes=56 * 2**20),
            name="multilevel",
        )
        table = jnp.asarray(TABLE, bf16)
        return call(charges.reshape(1024, 128), kernel_fine, kernel_mid, kernel_coarse, table).reshape(64, 16, 128)

    placed = (P("gx", "gy", None), P(), P(), P())
    return jax.shard_map(local, mesh=mesh, in_specs=placed, out_specs=P("gx", "gy", None), check_vma=False)
```

profile of v0, /device:TPU:1, one launch (start us, length us, event | category | flops | bytes accessed | tf_op | source)
XLA Modules:
  0.0 27.1 jit_solution(9128507206071311571)
XLA Ops:
  0.0 25.2 %multilevel.1 = f32[1024,128]{1,0:T(8,128)} custom-call(f32[1024,128]{1,0:T(8,128)} %bitcast.3, bf16[9,9,9]{2,1,0:T(8,128)(2,1)} %kf.1, bf16[9,9,9]{2,1,0:T(8,128)(2,1)} %km.1, bf16[9,9,9]{2,1,0:T(8,128)(2,1)} %kc.1, bf16[2480,128]{1,0:T(8,128)(2,1)} %constant.2.clone.const_hbm), custom_call_target="tpu_custom_call" | custom-call | tf_op jit(solution)/shard_map/multilevel/pallas_call | solution.py:395
  25.2 1.9 %copy.7 = f32[64,16,128]{2,1,0:T(8,128)} copy(f32[64,16,128]{2,1,0:T(8,128)} %bitcast.2) | data formatting | bytes 1048576
where the time goes:
time: 27.3 us; the launch traced here: 27.1 us
  Pallas kernels  25.2 us (92%)
  local copies, waits for them, and re-layouts  1.87 us (7%)
    pallas_call x1, Pallas kernels, local(): call(charges.reshape(1024, 128), kernel_fine, kernel_mid, kernel_coarse,...  25.2 us
    unnamed x1, local copies, waits for them, and re-layouts  1.87 us

commit v1 on v0

--- a/solution.py
+++ b/solution.py
@@ -13,7 +13,8 @@
 TAPS = {-3: -0.0625, -1: 0.5625, 0: 1.0, 1: 0.5625, 3: -0.0625}
 LEVELS = ((128, 1, 9), (64, 2, 10), (32, 4, 12))
 NEAR = ((0, -1), (0, 1), (-1, 0), (1, 0), (-1, -1), (-1, 1), (1, -1), (1, 1))
-FAR = tuple((i, j) for i in (-1, 0, 1) for j in (-2, -1, 0, 1, 2) if (i, j) != (0, 0))
+FAR = tuple((i, j) for i in (-1, 0, 1) for j in range(-3, 4) if (i, j) != (0, 0))
+QUADS = {-3: (0, 1), -2: (0, 2), -1: (0, 3), 0: (0, 3), 1: (0, 3), 2: (1, 3), 3: (2, 3)}
 
 
 def taps_matrix(fine, coarse):
@@ -42,7 +43,7 @@
     pieces["to_mid"] = to_mid
     rx = taps_matrix(range(64), mid_rows).T
     pieces["rx"] = np.concatenate([rx, rx], axis=1)
-    rc = taps_matrix(mid_rows, range(16)).T
+    rc = taps_matrix(mid_rows, [r - 6 for r in range(32)]).T
     pieces["rc"] = wide(np.concatenate([rc, rc], axis=1))
     pc = taps_matrix([o - 1 for o in range(48)], [i - 2 for i in range(32)])
     pc[35:] = 0.0
@@ -103,8 +104,8 @@
     return jnp.concatenate([table[dx, 128:128 + depth, :], table[dx, 0:depth, :]], axis=1)
 
 
-def body(sizes, c_hbm, kf, km, kc, const_hbm, out,
-         c, const, field, base_f, base_m, base_c, tab_f, tab_m, tab_c,
+def body(sizes, c_hbm, kf_hbm, km_hbm, kc_hbm, const_hbm, out,
+         c, const, kf, km, kc, field, base_f, base_m, base_c, tab_f, tab_m, tab_c,
          v_in, v_ed, fine, y_s, y_r, x_s, x_r, k_s, k_r, m_s, my_r, mx_r, mk_r,
          mid, coarse_s, coarse_r, coarse, u_ref,
          load_sem, fs_sem, fr_sem, ms_sem, mr_sem, cs_sem, cr_sem):
@@ -118,8 +119,8 @@
         x, y = gx - i, gy - j
         return (x >= 0) & (x < nx) & (y >= 0) & (y < ny)
 
-    def inside_columns(matrix, period, first, end):
-        place = lax.broadcasted_iota(jnp.int32, matrix.shape, 1) % period
+    def inside_x(matrix, axis, period, first, end):
+        place = lax.broadcasted_iota(jnp.int32, matrix.shape, axis) % period
         keep = ((place >= first) | (gx > 0)) & ((place < end) | (gx < nx - 1))
         return jnp.where(keep, matrix.astype(f32), 0.0).astype(bf16)
 
@@ -130,8 +131,12 @@
 
     load_c = pltpu.make_async_copy(c_hbm, c, load_sem.at[0])
     load_k = pltpu.make_async_copy(const_hbm, const, load_sem.at[1])
+    load_s = [pltpu.make_async_copy(source, target, load_sem.at[2 + n])
+              for n, (source, target) in enumerate(((kf_hbm, kf), (km_hbm, km), (kc_hbm, kc)))]
     load_c.start()
     load_k.start()
+    for load in load_s:
+        load.start()
     barrier = pltpu.get_barrier_semaphore()
     for i, j in FAR:
         pl.semaphore_signal(barrier, inc=1, device_id=device(i, j), device_id_type=MESH)
@@ -140,7 +145,6 @@
         start, rows = AT[name]
         return const[start:start + rows, 0:width]
 
-    toeplitz(kf, base_f, tab_f, 0, 128)
     load_c.wait()
     for y in range(16):
         for b in range(8):
@@ -177,12 +181,22 @@
     shares = dot(jnp.concatenate(highs, axis=0), table("block_z")) + dot(jnp.concatenate(lows, axis=0), table("block_z"))
     split = []
     for p in range(6):
-        high, low = high_low(shares[64 * p:64 * p + 64])
+        high, low = high_low(inside_y(shares[64 * p:64 * p + 64], (p == 5) - (p == 0)))
         split.append(jnp.concatenate([high, low], axis=0))
-    share = dot(table("rx"), jnp.concatenate(split, axis=1))
+    share = dot(inside_x(table("rx"), 0, 48, 8, 40), jnp.concatenate(split, axis=1))
     mid[...] = jnp.zeros_like(mid)
     mid[0:48, 256:1024] = share
     m_s[...] = share.astype(bf16)
+    high, low = high_low(share)
+    high, low = high_low(dot(inside_x(table("rc", 96), 0, 32, 6, 22), jnp.concatenate([high, low], axis=0)))
+    both = jnp.concatenate([high, low], axis=0)
+    weights = AT["to_coarse"][0]
+    coarse[...] = jnp.zeros_like(coarse)
+    for q, (p0, p1, m0) in enumerate(((0, 2, 5), (0, 6, 1), (3, 6, 0))):
+        part = dot(both[:, 128 * p0:128 * p1], const[weights + 128 * m0:weights + 128 * (m0 + p1 - p0), :])
+        part = inside_y(part[0:32] + part[32:64], q - 1)
+        coarse[0:32, 128 * q + 128:128 * q + 256] = part
+        coarse_s[:, 128 * q:128 * q + 128] = part.astype(bf16)
 
     pl.semaphore_wait(barrier, len(FAR))
     sends = []
@@ -194,7 +208,13 @@
         copy.start()
         return copy
 
-    fine_copies, mid_copies = [], []
+    fine_copies, mid_copies, coarse_copies = [], [], []
+    for n, (i, j) in enumerate(FAR):
+        q0, q1 = QUADS[j]
+        rows = pl.ds(0, 32) if i == 0 else pl.ds(0, 16) if i < 0 else pl.ds(16, 16)
+        columns = pl.ds(0, 128 * (q1 - q0))
+        coarse_copies.append(send(
+            coarse_s.at[rows, pl.ds(128 * q0, 128 * (q1 - q0))], coarse_r.at[n, rows, columns], cs_sem.at[n], cr_sem.at[n], i, j))
     for n, (i, j) in enumerate(NEAR):
         if i == 0:
             pair = (m_s.at[:, 0:512] if j < 0 else m_s.at[:, 256:768], my_r.at[n])
@@ -213,6 +233,9 @@
             pair = (k_s.at[n - 4], k_r.at[n - 4])
         fine_copies.append(send(*pair, fs_sem.at[n], fr_sem.at[n], i, j))
 
+    for load in load_s:
+        load.wait()
+    toeplitz(kf, base_f, tab_f, 0, 128)
     toeplitz(km, base_m, tab_m, 1, 128)
     toeplitz(kc, base_c, tab_c, 2, 0)
 
@@ -242,30 +265,6 @@
         r0, rows = (0, 48) if i == 0 else (32, 16) if i < 0 else (0, 16)
         l0, lanes = (256, 768) if j == 0 else (768, 512) if j < 0 else (0, 512)
         mid[r0:r0 + rows, l0:l0 + lanes] += got
-    @pl.when(gx == 0)
-    def _():
-        mid[0:8, :] = jnp.zeros((8, 1280), f32)
-
-    @pl.when(gx == nx - 1)
-    def _():
-        mid[40:48, :] = jnp.zeros((8, 1280), f32)
-
-    @pl.when(gy == 0)
-    def _():
-        mid[0:48, 0:384] = jnp.zeros((48, 384), f32)
-
-    @pl.when(gy == ny - 1)
-    def _():
-        mid[0:48, 896:1280] = jnp.zeros((48, 384), f32)
-
-    high, low = high_low(mid[0:48, 128:1024])
-    shrunk = dot(table("rc", 96), jnp.concatenate([high, low], axis=0))
-    high, low = high_low(shrunk)
-    own = dot(jnp.concatenate([high, low], axis=0), table("to_coarse"))
-    own = (own[0:16] + own[16:32]).astype(bf16)
-    coarse_s[...] = own
-    coarse_copies = [send(coarse_s, coarse_r.at[n], cs_sem.at[n], cr_sem.at[n], i, j) for n, (i, j) in enumerate(FAR)]
-
     for n in range(2):
         fine_copies[n].wait_recv()
         inside = from_inside(*NEAR[n])
@@ -311,14 +310,18 @@
         [jnp.concatenate([shifted[dx][:, 256 * g:256 * g + 768] for dx in range(9)], axis=1) for g in range(3)], axis=0)
     mid_potential = dot(left, weights)
 
-    coarse[48:56, :] = jnp.zeros((8, 640), f32)
-    coarse[16:32, 256:384] = own.astype(f32)
     for n, (i, j) in enumerate(FAR):
         coarse_copies[n].wait_recv()
-        coarse[16 - 16 * i:32 - 16 * i, 256 - 128 * j:384 - 128 * j] = jnp.where(
-            from_inside(i, j), coarse_r[n].astype(f32), 0.0)
+    for n, (i, j) in enumerate(FAR):
+        q0, q1 = QUADS[j]
+        r0, rows = (0, 32) if i == 0 else (16, 16) if i < 0 else (0, 16)
+        t0 = 0 if i <= 0 else 16
+        l0, lanes = 128 * (q0 + 1 - j), 128 * (q1 - q0)
+        got = coarse_r[n, t0:t0 + rows, 0:lanes].astype(f32)
+        coarse[r0:r0 + rows, l0:l0 + lanes] += jnp.where(from_inside(i, j), got, 0.0)
+
     weights = jnp.concatenate([tab_c[dx] for dx in range(9)], axis=0)
-    shifted = [coarse[10 + dx:42 + dx, :].astype(bf16) for dx in range(9)]
+    shifted = [coarse[dx:32 + dx, :].astype(bf16) for dx in range(9)]
     left = jnp.concatenate(
         [jnp.concatenate([shifted[dx][:, 128 * q:128 * q + 384] for dx in range(9)], axis=1) for q in range(3)], axis=0)
     coarse_potential = dot(left, weights)
@@ -326,7 +329,7 @@
     for q in range(3):
         high, low = high_low(inside_y(coarse_potential[32 * q:32 * q + 32], q - 1))
         split.append(jnp.concatenate([high, low], axis=0))
-    spread = dot(inside_columns(table("pc", 64), 32, 2, 18), jnp.concatenate(split, axis=1))
+    spread = dot(inside_x(table("pc", 64), 1, 32, 2, 18), jnp.concatenate(split, axis=1))
     high, low = high_low(spread)
     spread = jnp.concatenate([high, low], axis=0)
     to_mid = AT["to_mid"][0]
@@ -341,7 +344,7 @@
                 total = total + (part[0:48] + part[48:96])
         high, low = high_low(inside_y(total, -1 if p < 0 else 1 if p > 3 else 0))
         split.append(jnp.concatenate([high, low], axis=0))
-    along_x = dot(inside_columns(table("px", 96), 48, 1, 33), jnp.concatenate(split, axis=1))
+    along_x = dot(inside_x(table("px", 96), 1, 48, 1, 33), jnp.concatenate(split, axis=1))
     highs, lows = [], []
     for p in range(6):
         high, low = high_low(along_x[:, 128 * p:128 * p + 128])
@@ -366,16 +369,17 @@
 def solution(mesh):
     sizes = (mesh.shape["gx"], mesh.shape["gy"])
     vmem, dma = pltpu.VMEM, pltpu.SemaphoreType.DMA
-    in_vmem, anywhere = pl.BlockSpec(memory_space=pltpu.VMEM), pl.BlockSpec(memory_space=pl.ANY)
+    in_vmem, in_hbm = pl.BlockSpec(memory_space=pltpu.VMEM), pl.BlockSpec(memory_space=pltpu.HBM)
 
     def local(charges, kernel_fine, kernel_mid, kernel_coarse):
         call = pl.pallas_call(
             functools.partial(body, sizes),
             out_shape=jax.ShapeDtypeStruct((1024, 128), f32),
-            in_specs=[anywhere, in_vmem, in_vmem, in_vmem, anywhere],
+            in_specs=[in_hbm] * 5,
             out_specs=in_vmem,
             scratch_shapes=[
-                vmem((1024, 128), f32), vmem(TABLE.shape, bf16), vmem((24, 80, 128), f32),
+                vmem((1024, 128), f32), vmem(TABLE.shape, bf16),
+                vmem((9, 9, 9), bf16), vmem((9, 9, 9), bf16), vmem((9, 9, 9), bf16), vmem((24, 80, 128), f32),
                 vmem((9, 16, 128), f32), vmem((9, 16, 128), f32), vmem((9, 16, 128), f32),
                 vmem((9, 1408, 128), bf16), vmem((9, 896, 128), bf16), vmem((9, 384, 128), bf16),
                 vmem((9, 24, 48, 128), bf16), vmem((9, 24, 16, 128), bf16), vmem((16, 64, 128), f32),
@@ -383,9 +387,9 @@
                 vmem((2, 4, 16, 128), bf16), vmem((2, 4, 16, 128), bf16),
                 vmem((4, 32, 128), bf16), vmem((4, 32, 128), bf16),
                 vmem((48, 768), bf16), vmem((2, 48, 512), bf16), vmem((2, 16, 768), bf16), vmem((4, 16, 512), bf16),
-                vmem((64, 1280), f32), vmem((16, 128), bf16), vmem((14, 16, 128), bf16), vmem((56, 640), f32),
+                vmem((64, 1280), f32), vmem((32, 384), bf16), vmem((20, 32, 384), bf16), vmem((40, 640), f32),
                 vmem((12, 64, 128), f32),
-                dma((2,)), dma((8,)), dma((8,)), dma((8,)), dma((8,)), dma((14,)), dma((14,)),
+                dma((5,)), dma((8,)), dma((8,)), dma((8,)), dma((8,)), dma((20,)), dma((20,)),
             ],
             compiler_params=pltpu.CompilerParams(
                 collective_id=0, has_side_effects=True, vmem_limit_bytes=56 * 2**20),

time: 27.3 us -> 28.2 us (1.033)
  Pallas kernels: 25.2 us -> 26.2 us
    pallas_call x1, Pallas kernels: 25.2 us -> 26.2 us  [local(): call(charges.reshape(1024, 128), kernel_fine, kernel_mid, kernel_coarse,...]
where the time goes in v1:
time: 28.2 us; the launch traced here: 28.1 us
  Pallas kernels  26.2 us (93%)
  local copies, waits for them, and re-layouts  1.87 us (7%)
    pallas_call x1, Pallas kernels, local(): call(charges.reshape(1024, 128), kernel_fine, kernel_mid, kernel_coarse,...  26.2 us
    unnamed x1, local copies, waits for them, and re-layouts  1.87 us

profile of v1, /device:TPU:1, one launch (start us, length us, event | category | flops | bytes accessed | tf_op | source)
XLA Modules:
  0.0 28.1 jit_solution(472959268587050192)
XLA Ops:
  0.0 26.2 %multilevel.1 = f32[1024,128]{1,0:T(8,128)} custom-call(f32[1024,128]{1,0:T(8,128)} %bitcast.3, bf16[9,9,9]{2,1,0:T(8,128)(2,1)} %kf_hbm.1, bf16[9,9,9]{2,1,0:T(8,128)(2,1)} %km_hbm.1, bf16[9,9,9]{2,1,0:T(8,128)(2,1)} %kc_hbm.1, bf16[2496,128]{1,0:T(8,128)(2,1)} %constant.2.clone.const_hbm), custom_call_target="tpu_custom_call" | custom-call | tf_op jit(solution)/shard_map/multilevel/pallas_call | solution.py:399
  26.2 1.9 %copy.7 = f32[64,16,128]{2,1,0:T(8,128)} copy(f32[64,16,128]{2,1,0:T(8,128)} %bitcast.2) | data formatting | bytes 1048576

commit v2 on v1

--- a/solution.py
+++ b/solution.py
@@ -112,8 +112,14 @@
     gx, gy = lax.axis_index("gx"), lax.axis_index("gy")
     nx, ny = sizes
 
+    def wrapped(place, size):
+        return jnp.where(place < 0, place + size, jnp.where(place >= size, place - size, place))
+
+    along_gx = {i: wrapped(gx + i, nx) for i in (-1, 0, 1)}
+    along_gy = {j: wrapped(gy + j, ny) for j in range(-3, 4)}
+
     def device(i, j):
-        return (lax.rem(gx + i + nx, nx), lax.rem(gy + j + ny, ny))
+        return (along_gx[i], along_gy[j])
 
     def from_inside(i, j):
         x, y = gx - i, gy - j
@@ -209,12 +215,14 @@
         return copy
 
     fine_copies, mid_copies, coarse_copies = [], [], []
-    for n, (i, j) in enumerate(FAR):
-        q0, q1 = QUADS[j]
-        rows = pl.ds(0, 32) if i == 0 else pl.ds(0, 16) if i < 0 else pl.ds(16, 16)
-        columns = pl.ds(0, 128 * (q1 - q0))
-        coarse_copies.append(send(
-            coarse_s.at[rows, pl.ds(128 * q0, 128 * (q1 - q0))], coarse_r.at[n, rows, columns], cs_sem.at[n], cr_sem.at[n], i, j))
+    for n, (i, j) in enumerate(NEAR):
+        if i == 0:
+            pair = (y_s.at[n], y_r.at[n])
+        elif j == 0:
+            pair = (x_s.at[n - 2], x_r.at[n - 2])
+        else:
+            pair = (k_s.at[n - 4], k_r.at[n - 4])
+        fine_copies.append(send(*pair, fs_sem.at[n], fr_sem.at[n], i, j))
     for n, (i, j) in enumerate(NEAR):
         if i == 0:
             pair = (m_s.at[:, 0:512] if j < 0 else m_s.at[:, 256:768], my_r.at[n])
@@ -225,13 +233,12 @@
             columns = pl.ds(0, 512) if j < 0 else pl.ds(256, 512)
             pair = (m_s.at[rows, columns], mk_r.at[n - 4])
         mid_copies.append(send(*pair, ms_sem.at[n], mr_sem.at[n], i, j))
-        if i == 0:
-            pair = (y_s.at[n], y_r.at[n])
-        elif j == 0:
-            pair = (x_s.at[n - 2], x_r.at[n - 2])
-        else:
-            pair = (k_s.at[n - 4], k_r.at[n - 4])
-        fine_copies.append(send(*pair, fs_sem.at[n], fr_sem.at[n], i, j))
+    for n, (i, j) in enumerate(FAR):
+        q0, q1 = QUADS[j]
+        rows = pl.ds(0, 32) if i == 0 else pl.ds(0, 16) if i < 0 else pl.ds(16, 16)
+        columns = pl.ds(0, 128 * (q1 - q0))
+        coarse_copies.append(send(
+            coarse_s.at[rows, pl.ds(128 * q0, 128 * (q1 - q0))], coarse_r.at[n, rows, columns], cs_sem.at[n], cr_sem.at[n], i, j))
 
     for load in load_s:
         load.wait()
@@ -256,15 +263,6 @@
     fill_inside(range(4, 20))
     fine_inside((2, 3, 4, 5))
 
-    for n, (i, j) in enumerate(NEAR):
-        mid_copies[n].wait_recv()
-    for n, (i, j) in enumerate(NEAR):
-        inside = from_inside(i, j)
-        got = my_r[n] if i == 0 else mx_r[n - 2] if j == 0 else mk_r[n - 4]
-        got = jnp.where(inside, got.astype(f32), 0.0)
-        r0, rows = (0, 48) if i == 0 else (32, 16) if i < 0 else (0, 16)
-        l0, lanes = (256, 768) if j == 0 else (768, 512) if j < 0 else (0, 512)
-        mid[r0:r0 + rows, l0:l0 + lanes] += got
     for n in range(2):
         fine_copies[n].wait_recv()
         inside = from_inside(*NEAR[n])
@@ -304,6 +302,15 @@
             fine[2 * q + k, 0:8, :] = piece[0:8]
             fine[2 * q + k, 56:64, :] = piece[8:16]
 
+    for n, (i, j) in enumerate(NEAR):
+        mid_copies[n].wait_recv()
+    for n, (i, j) in enumerate(NEAR):
+        inside = from_inside(i, j)
+        got = my_r[n] if i == 0 else mx_r[n - 2] if j == 0 else mk_r[n - 4]
+        got = jnp.where(inside, got.astype(f32), 0.0)
+        r0, rows = (0, 48) if i == 0 else (32, 16) if i < 0 else (0, 16)
+        l0, lanes = (256, 768) if j == 0 else (768, 512) if j < 0 else (0, 512)
+        mid[r0:r0 + rows, l0:l0 + lanes] += got
     weights = jnp.concatenate([wide_table(tab_m, dx, 768) for dx in range(9)], axis=0)
     shifted = [mid[3 + dx:51 + dx, :].astype(bf16) for dx in range(9)]
     left = jnp.concatenate(

time: 28.2 us -> 24 us (0.85)
  Pallas kernels: 26.2 us -> 22 us
    pallas_call x1, Pallas kernels: 26.2 us -> 22 us  [local(): call(charges.reshape(1024, 128), kernel_fine, kernel_mid, kernel_coarse,...]
where the time goes in v2:
time: 24 us; the launch traced here: 23.9 us
  Pallas kernels  22 us (92%)
  local copies, waits for them, and re-layouts  1.87 us (8%)
    pallas_call x1, Pallas kernels, local(): call(charges.reshape(1024, 128), kernel_fine, kernel_mid, kernel_coarse,...  22 us
    unnamed x1, local copies, waits for them, and re-layouts  1.87 us

profile of v2, /device:TPU:1, one launch (start us, length us, event | category | flops | bytes accessed | tf_op | source)
XLA Modules:
  0.0 23.9 jit_solution(375136420687530097)
XLA Ops:
  0.0 22.0 %multilevel.1 = f32[1024,128]{1,0:T(8,128)} custom-call(f32[1024,128]{1,0:T(8,128)} %bitcast.3, bf16[9,9,9]{2,1,0:T(8,128)(2,1)} %kf_hbm.1, bf16[9,9,9]{2,1,0:T(8,128)(2,1)} %km_hbm.1, bf16[9,9,9]{2,1,0:T(8,128)(2,1)} %kc_hbm.1, bf16[2496,128]{1,0:T(8,128)(2,1)} %constant.2.clone.const_hbm), custom_call_target="tpu_custom_call" | custom-call | tf_op jit(solution)/shard_map/multilevel/pallas_call | solution.py:406
  22.0 1.9 %copy.7 = f32[64,16,128]{2,1,0:T(8,128)} copy(f32[64,16,128]{2,1,0:T(8,128)} %bitcast.2) | data formatting | bytes 1048576
